TPU v7x, 32 devices: a whole 2x2x4 slice. The times are simulated.
32 devices in a mesh: prow: 8 (over y, x, core), pcol: 4 (over z).
Axes of the slice: x: 2, y: 2, z: 4, core: 2. Of those that a mesh axis runs over, the one named last changes fastest.
Arguments:
- cov_trail: float32 [1024, 1024], P('prow', 'pcol'), as said below
- factor_panel: bfloat16 [4, 1024, 128], P(None, 'prow'), may hold values from -0.25 to 0.25
- first_level: int32 [8], replicated, may hold values from 0 to 4
- block_slot: int32 [8], replicated, may hold values from 0 to 7, each once
- factor_window: bfloat16 [6, 128, 128], replicated, may hold values from -0.5 to 0.5
- diag_inverse: float32 [4, 128, 128], replicated, as said below
Outputs:
- panel_cov: float32 [4, 1024, 128], P(None, 'prow')
- window_cov: float32 [512, 512], replicated
Inputs may be any that keep to these rules, and one draw needn't show every extreme that they name: Trailing block j lies in the pattern of window supernode k exactly when first_level[j] <= k, so the patterns are nested. `block_slot`: a permutation; slot s is held by process row s // 1 and process column s // (8 / pcol size), slots in contiguous blocks. `cov_trail`: symmetric. `diag_inverse`: each block symmetric.
All inputs are finite; a program needn't handle non-finite values.
Results may differ from a plain program's by a relative error of at most 0.0003.
Values may be sent and summed in bfloat16 or wider, within the bound.
A program may use at most 64 MiB of HBM per device.

v0:
```python
import jax
import jax.numpy as jnp
from jax import lax
from jax.sharding import PartitionSpec as P


def pair_index(upper, lower, window_count):
    return lower * window_count - lower * (lower + 1) // 2 + upper - lower - 1


def later_block(window, upper, lower):
    if upper >= lower:
        return window[upper, lower]
    return window[lower, upper].T


def window_step(window, cross_sums, diag_term, later_nodes, window_factor, diag_block, supernode):
    highest = lax.Precision.HIGHEST
    for place, upper in enumerate(later_nodes):
        block_total = cross_sums[place]
        for second, other in enumerate(later_nodes):
            block_total = block_total + jnp.dot(
                later_block(window, upper, other),
                window_factor[second],
                precision=highest,
                preferred_element_type=jnp.float32,
            )
        window[upper, supernode] = -block_total
    diagonal = diag_block - diag_term
    for place, upper in enumerate(later_nodes):
        diagonal = diagonal - jnp.dot(
            window_factor[place].T,
            window[upper, supernode],
            precision=highest,
            preferred_element_type=jnp.float32,
        )
    window[supernode, supernode] = diagonal


def shards(cov_trail, factor_panel, first_level, block_slot, factor_window, diag_inverse):
    highest = lax.Precision.HIGHEST
    block_size = diag_inverse.shape[-1]
    window_count = diag_inverse.shape[0]
    rows_loc = cov_trail.shape[0]
    cols_loc = cov_trail.shape[1]
    block_count = first_level.shape[0]
    slot_ids = lax.iota(jnp.int32, block_count)
    level_slot = jnp.sum(
        jnp.where(block_slot[None, :] == slot_ids[:, None], first_level[None, :], 0), axis=1
    )
    local_blocks = rows_loc // block_size
    row_level = jnp.repeat(
        lax.dynamic_slice_in_dim(level_slot, lax.axis_index("prow") * local_blocks, local_blocks),
        block_size,
    )
    columns = {}
    window = {}
    for supernode in range(window_count - 1, -1, -1):
        keep_rows = (row_level <= supernode)[:, None]
        panel_row = jnp.where(keep_rows, factor_panel[supernode], jnp.zeros((), jnp.bfloat16))
        gathered = lax.all_gather(panel_row, "prow", axis=0, tiled=True)
        panel_col = lax.dynamic_slice_in_dim(
            gathered, lax.axis_index("pcol") * cols_loc, cols_loc, 0
        )
        panel_full = panel_row.astype(jnp.float32)
        partial_prod = jnp.dot(
            cov_trail,
            panel_col.astype(jnp.float32),
            precision=highest,
            preferred_element_type=jnp.float32,
        )
        later_nodes = list(range(supernode + 1, window_count))
        window_factor = [
            factor_window[pair_index(upper, supernode, window_count)].astype(jnp.float32)
            for upper in later_nodes
        ]
        summed = lax.psum(partial_prod, "pcol")
        accumulated = summed
        for place, upper in enumerate(later_nodes):
            accumulated = accumulated + jnp.dot(
                columns[upper],
                window_factor[place],
                precision=highest,
                preferred_element_type=jnp.float32,
            )
        new_column = jnp.where(keep_rows, -accumulated, jnp.float32(0.0))
        columns[supernode] = new_column
        term_list = []
        for upper in later_nodes:
            term_list.append(
                jnp.dot(
                    columns[upper].T,
                    panel_full,
                    precision=highest,
                    preferred_element_type=jnp.float32,
                )
            )
        term_list.append(
            jnp.dot(panel_full.T, new_column, precision=highest, preferred_element_type=jnp.float32)
        )
        cross_sums = lax.psum(jnp.stack(term_list), "prow")
        diag_term = cross_sums[len(later_nodes)]
        window_step(
            window,
            cross_sums,
            diag_term,
            later_nodes,
            window_factor,
            diag_inverse[supernode],
            supernode,
        )
    panel_cov = jnp.stack([columns[supernode] for supernode in range(window_count)])
    block_rows = [
        jnp.concatenate(
            [later_block(window, upper, other) for other in range(window_count)], axis=1
        )
        for upper in range(window_count)
    ]
    window_cov = jnp.concatenate(block_rows, axis=0)
    return (panel_cov, window_cov)


def solution(mesh):
    return jax.shard_map(
        shards,
        mesh=mesh,
        in_specs=(P("prow", "pcol"), P(None, "prow", None), P(), P(), P(), P()),
        out_specs=(P(None, "prow", None), P()),
        check_vma=False,
    )
```

profile of v0, /device:TPU:0, one launch (start us, length us, event | category | flops | bytes accessed | tf_op | source)
XLA Modules:
  0.0 169.3 jit_solution(11450177156620109265)
XLA Ops:
  7.3 0.7 copy-done.9
  8.0 0.6 dynamic_slice.15
  11.2 0.8 slice_select_fusion.3
  12.1 10.8 %all-gather.3 = bf16[1,1024,128]{2,1,0:T(8,128)(2,1)S(1)} all-gather(bf16[1,128,128]{2,1,0:T(8,128)(2,1)S(1)} %get-tuple-element.20), channel_id=5, replica_groups=mesh['prow'=8,'pcol'=4] {'prow'}, dimensions={1}, use_global_device_ids=true | all-gather | bytes 294912 | tf_op jit(solution)/shard_map/all_gather | solution.py:61
  22.8 9.3 %all-gather.2 = bf16[1,1024,128]{2,1,0:T(8,128)(2,1)S(1)} all-gather(bf16[1,128,128]{2,1,0:T(8,128)(2,1)S(1)} %get-tuple-element.21), channel_id=4, replica_groups=mesh['prow'=8,'pcol'=4] {'prow'}, dimensions={1}, use_global_device_ids=true | all-gather | bytes 294912 | tf_op jit(solution)/shard_map/all_gather | solution.py:61
  32.1 0.9 convolution_bitcast_fusion.16
  33.0 0.9 convolution_bitcast_fusion.17
  33.9 8.3 %all-gather.1 = bf16[1,1024,128]{2,1,0:T(8,128)(2,1)S(1)} all-gather(bf16[1,128,128]{2,1,0:T(8,128)(2,1)S(1)} %get-tuple-element.19), channel_id=3, replica_groups=mesh['prow'=8,'pcol'=4] {'prow'}, dimensions={1}, use_global_device_ids=true | all-gather | bytes 294912 | tf_op jit(solution)/shard_map/all_gather | solution.py:61
  42.2 0.9 convolution_bitcast_fusion.18
  43.1 9.3 %all-gather = bf16[1,1024,128]{2,1,0:T(8,128)(2,1)S(1)} all-gather(bf16[1,128,128]{2,1,0:T(8,128)(2,1)S(1)} %get-tuple-element.18), channel_id=2, replica_groups=mesh['prow'=8,'pcol'=4] {'prow'}, dimensions={1}, use_global_device_ids=true | all-gather | bytes 294912 | tf_op jit(solution)/shard_map/all_gather | solution.py:61
  52.4 0.9 convolution_bitcast_fusion.19
  53.3 36.4 %all-reduce.7.cloned.1.call-done = (f32[128,128]{0,1:T(8,128)}, f32[128,128]{0,1:T(8,128)}, f32[128,128]{0,1:T(8,128)}, f32[128,128]{0,1:T(8,128)}) async-done(((f32[128,128]{0,1:T(8,128)}, f32[128,128]{0,1:T(8,128)}, f32[128,128]{0,1:T(8,128)}, f32[128,128]{0,1:T(8,128)}), (f32[128,128]{0,1:T(8,128)}, f32[128,128]{0,1:T(8,128)}, f32[128,128]{0,1:T(8,128)}, ...) | async-done | bytes 262160 | tf_op jit(solution)/shard_map/psum | solution.py:77
  89.7 1.1 fusion.17
  91.2 0.6 copy-done.1
  93.6 1.7 convolution_bitcast_fusion.6
  95.7 0.2 fusion.13
  96.2 0.7 pad_maximum_fusion.4
  96.9 0.7 pad_maximum_fusion.3
  97.5 0.7 pad_maximum_fusion.1
  98.3 0.8 copy.67
  99.2 54.7 %all-reduce.5.cloned.1.call-done = (f32[1,128,128]{2,1,0:T(8,128)}, f32[2,128,128]{1,2,0:T(8,128)}, f32[3,128,128]{2,1,0:T(8,128)}, f32[4,128,128]{2,1,0:T(8,128)}) async-done(((f32[1,128,128]{2,1,0:T(8,128)}, f32[2,128,128]{1,2,0:T(8,128)}, f32[3,128,128]{2,1,0:T(8,128)}, f32[4,128,128]{2,1,0:T(8,128)}), (f32[1,128,128]{2,1,0:T(8,128)}, f32[2,128,128]{1,2,0:T(8,128)}, f32[3,128,128]{2,1,0:T(8,128)}, ...) | async-done | bytes 655376 | tf_op jit(solution)/shard_map/psum | solution.py:101
  153.8 1.0 fusion.103
  155.2 0.6 copy-done.5
  155.7 0.2 convolution_add_fusion.10
  156.4 0.2 convolution_add_fusion.12
  156.9 0.4 copy-done.3
  157.5 0.2 convolution_add_fusion.1
  158.9 0.2 convolution_add_fusion.8
  159.4 0.2 fusion.5
  160.4 0.2 fusion.3
  160.7 0.2 fusion.2
  161.4 1.1 maximum_maximum_fusion
  (61 shorter events, 6.7 us)
Async XLA Ops:
  7.2 24.9 %copy-start = (f32[128,256]{1,0:T(8,128)S(1)}, f32[128,256]{1,0:T(8,128)}, u32[]{:S(2)}) copy-start(f32[128,256]{1,0:T(8,128)} %param.6) | copy-start | bytes 393220
  7.2 82.6 %all-reduce.7.cloned.1.call-start = ((), (), s32[]{:S(2)}) async-start(), calls=%async_computation.1 | async-start | bytes 524288 | tf_op jit(solution)/shard_map/psum | solution.py:77
  7.2 0.7 copy-start.9
  7.2 0.7 copy-start.10
  53.3 36.5 %copy-start.2 = (bf16[6,128,128]{2,1,0:T(8,128)(2,1)S(1)}, bf16[6,128,128]{2,1,0:T(8,128)(2,1)}, u32[]{:S(2)}) copy-start(bf16[6,128,128]{2,1,0:T(8,128)(2,1)} %param.10) | copy-start | bytes 589828
  53.3 100.6 %all-reduce.5.cloned.1.call-start = ((), (), s32[]{:S(2)}) async-start(), calls=%async_computation | async-start | bytes 1310720 | tf_op jit(solution)/shard_map/psum | solution.py:101
  89.7 1.2 copy-start.8
  90.9 0.8 copy-start.1
  93.6 1.7 copy-start.7
  98.3 55.5 %copy-start.4 = (f32[4,128,128]{2,1,0:T(8,128)S(1)}, f32[4,128,128]{2,1,0:T(8,128)}, u32[]{:S(2)}) copy-start(f32[4,128,128]{2,1,0:T(8,128)} %param.11) | copy-start | bytes 786436
  153.8 1.0 copy-start.6
  154.8 0.9 copy-start.5
  156.4 1.0 copy-start.3
Sparse Core Ops, SparseCore 0:
  53.4 36.2 all-reduce.6
  98.4 55.3 all-reduce.4
where the time goes:
time: 170 us; the launch traced here: 169 us
  waiting for transfers between devices  91.1 us (54%)
  blocking collectives  37.6 us (22%)
  between operations  17.1 us (10%)
  matrix products  13.7 us (8%)
  other arithmetic  5.08 us (3%)
  local copies, waits for them, and re-layouts  4.56 us (3%)
    psum x1, waiting for transfers between devices, shards(): cross_sums = lax.psum(jnp.stack(term_list), 'prow')  54.7 us
    all_gather x4, blocking collectives, shards(): gathered = lax.all_gather(panel_row, 'prow', axis=0, tiled=True)  37.6 us
    psum x1, waiting for transfers between devices, shards(): summed = lax.psum(partial_prod, 'pcol')  36.4 us
    dot_general x4, matrix products, shards(): jnp.dot(cov_trail, panel_col.astype(jnp.float32), precision=highest, pref...  3.55 us
    unnamed x26, local copies, waits for them, and re-layouts  3.41 us
  transfers between devices with their start and end apart: 2, of which 2 were waited for; matrix products, arithmetic and copies ran while one was open for 1% of the time, Pallas kernels for 0%

commit v1 on v0

--- a/solution.py
+++ b/solution.py
@@ -2,6 +2,24 @@
 import jax.numpy as jnp
 from jax import lax
 from jax.sharding import PartitionSpec as P
+
+
+def in_order(blocks, dim):
+    blocks = jnp.moveaxis(blocks, 0, dim)
+    shape = blocks.shape
+    return blocks.reshape(*shape[:dim], shape[dim] * shape[dim + 1], *shape[dim + 2 :])
+
+
+def doubled(array, axis):
+    size = lax.axis_size(axis)
+    parts = array[None]
+    for level in range(size.bit_length() - 1):
+        distance = 1 << level
+        partner_block = lax.ppermute(parts, axis, [(i, i ^ distance) for i in range(size)])
+        both = jnp.stack([parts, partner_block])
+        upper = lax.axis_index(axis) >> level & 1
+        parts = jnp.where(upper == 0, both, both[::-1]).reshape(-1, *array.shape)
+    return parts
 
 
 def pair_index(upper, lower, window_count):
@@ -58,7 +76,7 @@
     for supernode in range(window_count - 1, -1, -1):
         keep_rows = (row_level <= supernode)[:, None]
         panel_row = jnp.where(keep_rows, factor_panel[supernode], jnp.zeros((), jnp.bfloat16))
-        gathered = lax.all_gather(panel_row, "prow", axis=0, tiled=True)
+        gathered = in_order(doubled(panel_row, "prow"), 0)
         panel_col = lax.dynamic_slice_in_dim(
             gathered, lax.axis_index("pcol") * cols_loc, cols_loc, 0
         )

time: 170 us -> 156 us (0.918)
  blocking collectives: 37.6 us -> 0 us
  waiting for transfers between devices: 91.1 us -> 104 us
  starting transfers between devices: 0.08 us -> 10.3 us
    all_gather x4 -> x0, blocking collectives: 37.6 us -> none  [shards(): gathered = lax.all_gather(panel_row, 'prow', axis=0, tiled=True)]
    ppermute x0 -> x12, waiting for transfers between devices: none -> 11.7 us  [doubled(): lax.ppermute(parts, axis, [(i, i ^ distance) for i in range(size)])]
    ppermute x0 -> x12, starting transfers between devices: none -> 10.2 us  [doubled(): lax.ppermute(parts, axis, [(i, i ^ distance) for i in range(size)])]
    unnamed x26 -> x28, local copies, waits for them, and re-layouts: 3.41 us -> 4.06 us
  transfers between devices with their start and end apart: 2 -> 14, of which waited for: 2 -> 11; matrix products, arithmetic and copies ran while one was open for 1% -> 3% of each run, Pallas kernels for 0% -> 0%
where the time goes in v1:
time: 156 us
  waiting for transfers between devices  104 us (67%)
  between operations  17.2 us (11%)
  matrix products  13 us (8%)
  starting transfers between devices  10.3 us (7%)
  other arithmetic  5.69 us (4%)
  local copies, waits for them, and re-layouts  5.21 us (3%)
    psum x1, waiting for transfers between devices, shards(): cross_sums = lax.psum(jnp.stack(term_list), 'prow')  54.7 us
    psum x1, waiting for transfers between devices, shards(): summed = lax.psum(partial_prod, 'pcol')  37.8 us
    ppermute x12, waiting for transfers between devices, doubled(): lax.ppermute(parts, axis, [(i, i ^ distance) for i in range(size)])  11.7 us
    ppermute x12, starting transfers between devices, doubled(): lax.ppermute(parts, axis, [(i, i ^ distance) for i in range(size)])  10.2 us
    unnamed x28, local copies, waits for them, and re-layouts  4.06 us
    dot_general x4, matrix products, shards(): jnp.dot(cov_trail, panel_col.astype(jnp.float32), precision=highest, pref...  3.56 us
  transfers between devices with their start and end apart: 14, of which 11 were waited for; matrix products, arithmetic and copies ran while one was open for 3% of the time, Pallas kernels for 0%

profile of v1, /device:TPU:0, one launch (start us, length us, event | category | flops | bytes accessed | tf_op | source)
XLA Modules:
  0.0 155.5 jit_solution(12669768431566766794)
XLA Ops:
  7.3 0.7 copy-done.10
  8.0 0.6 dynamic_slice.15
  11.2 0.8 slice_select_fusion.3
  12.1 0.5 collective-permute-start.3
  13.4 0.9 collective-permute-done
  14.4 2.7 %collective-permute-start.7 = (bf16[2,128,128]{2,1,0:T(8,128)(2,1)S(1)}, bf16[2,128,128]{2,1,0:T(8,128)(2,1)S(1)}, u32[]{:S(2)}, u32[]{:S(2)}) collective-permute-start(bf16[2,128,128]{2,1,0:T(8,128)(2,1)S(1)} %get-tuple-element.27), channel_id=1, source_target_pairs={{0,8},{4,12},{8,0},{12,4},{16,24},{20,28},{24,16},{28,20},{1,9},{5... | collective-permute-start | bytes 196616 | tf_op jit(solution)/shard_map/ppermute | solution.py:18
  17.3 2.0 %collective-permute-start.4 = (bf16[2,128,128]{2,1,0:T(8,128)(2,1)S(1)}, bf16[2,128,128]{2,1,0:T(8,128)(2,1)S(1)}, u32[]{:S(2)}, u32[]{:S(2)}) collective-permute-start(bf16[2,128,128]{2,1,0:T(8,128)(2,1)S(1)} %get-tuple-element.25), channel_id=1, source_target_pairs={{0,8},{4,12},{8,0},{12,4},{16,24},{20,28},{24,16},{28,20},{1,9},{5... | collective-permute-start | bytes 196616 | tf_op jit(solution)/shard_map/ppermute | solution.py:18
  19.8 3.6 %collective-permute-done.4 = bf16[2,128,128]{2,1,0:T(8,128)(2,1)S(1)} collective-permute-done((bf16[2,128,128]{2,1,0:T(8,128)(2,1)S(1)}, bf16[2,128,128]{2,1,0:T(8,128)(2,1)S(1)}, u32[]{:S(2)}, u32[]{:S(2)}) %collective-permute-start.4) | collective-permute-done | bytes 65568 | tf_op jit(solution)/shard_map/ppermute | solution.py:18
  23.5 0.6 collective-permute-done.1
  24.2 1.7 %collective-permute-start.2 = (bf16[4,128,128]{2,1,0:T(8,128)(2,1)S(1)}, bf16[4,128,128]{2,1,0:T(8,128)(2,1)S(1)}, u32[]{:S(2)}, u32[]{:S(2)}) collective-permute-start(bf16[4,128,128]{2,1,0:T(8,128)(2,1)S(1)} %bitcast.284), channel_id=1, source_target_pairs={{0,16},{4,20},{8,24},{12,28},{16,0},{20,4},{24,8},{28,12},{1,17},{... | collective-permute-start | bytes 393224 | tf_op jit(solution)/shard_map/ppermute | solution.py:18
  25.8 0.4 collective-permute-start.5
  26.3 1.6 %collective-permute-start.8 = (bf16[4,128,128]{2,1,0:T(8,128)(2,1)S(1)}, bf16[4,128,128]{2,1,0:T(8,128)(2,1)S(1)}, u32[]{:S(2)}, u32[]{:S(2)}) collective-permute-start(bf16[4,128,128]{2,1,0:T(8,128)(2,1)S(1)} %bitcast.278), channel_id=1, source_target_pairs={{0,16},{4,20},{8,24},{12,28},{16,0},{20,4},{24,8},{28,12},{1,17},{... | collective-permute-start | bytes 393224 | tf_op jit(solution)/shard_map/ppermute | solution.py:18
  27.9 0.5 collective-permute-start.11
  28.4 2.2 %collective-permute-done.2 = bf16[4,128,128]{2,1,0:T(8,128)(2,1)S(1)} collective-permute-done((bf16[4,128,128]{2,1,0:T(8,128)(2,1)S(1)}, bf16[4,128,128]{2,1,0:T(8,128)(2,1)S(1)}, u32[]{:S(2)}, u32[]{:S(2)}) %collective-permute-start.2) | collective-permute-done | bytes 131104 | tf_op jit(solution)/shard_map/ppermute | solution.py:18
  30.7 2.7 %collective-permute-done.5 = bf16[4,128,128]{2,1,0:T(8,128)(2,1)S(1)} collective-permute-done((bf16[4,128,128]{2,1,0:T(8,128)(2,1)S(1)}, bf16[4,128,128]{2,1,0:T(8,128)(2,1)S(1)}, u32[]{:S(2)}, u32[]{:S(2)}) %collective-permute-start.5) | collective-permute-done | bytes 131104 | tf_op jit(solution)/shard_map/ppermute | solution.py:18
  33.5 0.9 convolution_bitcast_fusion.19
  34.4 0.9 convolution_bitcast_fusion.18
  35.3 0.6 collective-permute-done.8
  36.0 0.9 convolution_bitcast_fusion.17
  37.4 0.9 convolution_bitcast_fusion.16
  38.4 37.8 %all-reduce.7.cloned.1.call-done = (f32[128,128]{0,1:T(8,128)}, f32[128,128]{0,1:T(8,128)}, f32[128,128]{0,1:T(8,128)}, f32[128,128]{0,1:T(8,128)}) async-done(((f32[128,128]{0,1:T(8,128)}, f32[128,128]{0,1:T(8,128)}, f32[128,128]{0,1:T(8,128)}, f32[128,128]{0,1:T(8,128)}), (f32[128,128]{0,1:T(8,128)}, f32[128,128]{0,1:T(8,128)}, f32[128,128]{0,1:T(8,128)}, ...) | async-done | bytes 262160 | tf_op jit(solution)/shard_map/psum | solution.py:95
  76.1 1.8 %convolution_bitcast_fusion.6 = f32[1,128,128]{2,1,0:T(8,128)} fusion(bf16[1,128,128]{2,1,0:T(8,128)(2,1)S(1)} %get-tuple-element.20, f32[128,128]{0,1:T(8,128)} %get-tuple-element.10, pred[]{:T(512)} %bitcast.33), kind=kOutput, calls=%fused_computation.32 | convolution fusion | flops 25198592 | bytes 163841 | tf_op jit(solution)/shard_map/dot_general | solution.py:117
  78.2 0.6 copy-done.8
  80.8 0.6 copy-done.7
  82.5 0.7 pad_maximum_fusion.12
  83.1 0.7 pad_maximum_fusion.7
  83.8 0.7 pad_maximum_fusion.5
  84.6 0.8 copy.71
  85.4 54.7 %all-reduce.5.cloned.1.call-done = (f32[1,128,128]{2,1,0:T(8,128)}, f32[2,128,128]{1,2,0:T(8,128)}, f32[3,128,128]{2,1,0:T(8,128)}, f32[4,128,128]{2,1,0:T(8,128)}) async-done(((f32[1,128,128]{2,1,0:T(8,128)}, f32[2,128,128]{1,2,0:T(8,128)}, f32[3,128,128]{2,1,0:T(8,128)}, f32[4,128,128]{2,1,0:T(8,128)}), (f32[1,128,128]{2,1,0:T(8,128)}, f32[2,128,128]{1,2,0:T(8,128)}, f32[3,128,128]{2,1,0:T(8,128)}, ...) | async-done | bytes 655376 | tf_op jit(solution)/shard_map/psum | solution.py:119
  140.1 1.0 fusion.107
  141.4 0.6 copy-done.5
  147.6 1.1 maximum_maximum_fusion
  (107 shorter events, 11.7 us)
Async XLA Ops:
  7.2 26.4 %copy-start = (f32[128,256]{1,0:T(8,128)S(1)}, f32[128,256]{1,0:T(8,128)}, u32[]{:S(2)}) copy-start(f32[128,256]{1,0:T(8,128)} %param.6) | copy-start | bytes 393220
  7.2 69.0 %all-reduce.7.cloned.1.call-start = ((), (), s32[]{:S(2)}) async-start(), calls=%async_computation.1 | async-start | bytes 524288 | tf_op jit(solution)/shard_map/psum | solution.py:95
  7.2 0.7 copy-start.10
  7.2 0.7 copy-start.11
  12.1 1.4 collective-permute-start.3
  12.6 4.6 %collective-permute-start.9 = (bf16[1,128,128]{2,1,0:T(8,128)(2,1)S(1)}, bf16[1,128,128]{2,1,0:T(8,128)(2,1)S(1)}, u32[]{:S(2)}, u32[]{:S(2)}) collective-permute-start(bf16[1,128,128]{2,1,0:T(8,128)(2,1)S(1)} %get-tuple-element.20), channel_id=1, source_target_pairs={{0,4},{4,0},{8,12},{12,8},{16,20},{20,16},{24,28},{28,24},{1,5},{5... | collective-permute-start | bytes 98312 | tf_op jit(solution)/shard_map/ppermute | solution.py:18
  12.7 1.7 %collective-permute-start.6 = (bf16[1,128,128]{2,1,0:T(8,128)(2,1)S(1)}, bf16[1,128,128]{2,1,0:T(8,128)(2,1)S(1)}, u32[]{:S(2)}, u32[]{:S(2)}) collective-permute-start(bf16[1,128,128]{2,1,0:T(8,128)(2,1)S(1)} %get-tuple-element.21), channel_id=1, source_target_pairs={{0,4},{4,0},{8,12},{12,8},{16,20},{20,16},{24,28},{28,24},{1,5},{5... | collective-permute-start | bytes 98312 | tf_op jit(solution)/shard_map/ppermute | solution.py:18
  13.1 1.2 collective-permute-start
  14.4 5.3 %collective-permute-start.7 = (bf16[2,128,128]{2,1,0:T(8,128)(2,1)S(1)}, bf16[2,128,128]{2,1,0:T(8,128)(2,1)S(1)}, u32[]{:S(2)}, u32[]{:S(2)}) collective-permute-start(bf16[2,128,128]{2,1,0:T(8,128)(2,1)S(1)} %get-tuple-element.27), channel_id=1, source_target_pairs={{0,8},{4,12},{8,0},{12,4},{16,24},{20,28},{24,16},{28,20},{1,9},{5... | collective-permute-start | bytes 196616 | tf_op jit(solution)/shard_map/ppermute | solution.py:18
  17.2 10.7 %collective-permute-start.10 = (bf16[2,128,128]{2,1,0:T(8,128)(2,1)S(1)}, bf16[2,128,128]{2,1,0:T(8,128)(2,1)S(1)}, u32[]{:S(2)}, u32[]{:S(2)}) collective-permute-start(bf16[2,128,128]{2,1,0:T(8,128)(2,1)S(1)} %get-tuple-element.29), channel_id=1, source_target_pairs={{0,8},{4,12},{8,0},{12,4},{16,24},{20,28},{24,16},{28,20},{1,9},{5... | collective-permute-start | bytes 196616 | tf_op jit(solution)/shard_map/ppermute | solution.py:18
  17.3 6.2 %collective-permute-start.4 = (bf16[2,128,128]{2,1,0:T(8,128)(2,1)S(1)}, bf16[2,128,128]{2,1,0:T(8,128)(2,1)S(1)}, u32[]{:S(2)}, u32[]{:S(2)}) collective-permute-start(bf16[2,128,128]{2,1,0:T(8,128)(2,1)S(1)} %get-tuple-element.25), channel_id=1, source_target_pairs={{0,8},{4,12},{8,0},{12,4},{16,24},{20,28},{24,16},{28,20},{1,9},{5... | collective-permute-start | bytes 196616 | tf_op jit(solution)/shard_map/ppermute | solution.py:18
  19.3 4.9 %collective-permute-start.1 = (bf16[2,128,128]{2,1,0:T(8,128)(2,1)S(1)}, bf16[2,128,128]{2,1,0:T(8,128)(2,1)S(1)}, u32[]{:S(2)}, u32[]{:S(2)}) collective-permute-start(bf16[2,128,128]{2,1,0:T(8,128)(2,1)S(1)} %get-tuple-element.23), channel_id=1, source_target_pairs={{0,8},{4,12},{8,0},{12,4},{16,24},{20,28},{24,16},{28,20},{1,9},{5... | collective-permute-start | bytes 196616 | tf_op jit(solution)/shard_map/ppermute | solution.py:18
  24.2 6.4 %collective-permute-start.2 = (bf16[4,128,128]{2,1,0:T(8,128)(2,1)S(1)}, bf16[4,128,128]{2,1,0:T(8,128)(2,1)S(1)}, u32[]{:S(2)}, u32[]{:S(2)}) collective-permute-start(bf16[4,128,128]{2,1,0:T(8,128)(2,1)S(1)} %bitcast.284), channel_id=1, source_target_pairs={{0,16},{4,20},{8,24},{12,28},{16,0},{20,4},{24,8},{28,12},{1,17},{... | collective-permute-start | bytes 393224 | tf_op jit(solution)/shard_map/ppermute | solution.py:18
  25.8 7.6 %collective-permute-start.5 = (bf16[4,128,128]{2,1,0:T(8,128)(2,1)S(1)}, bf16[4,128,128]{2,1,0:T(8,128)(2,1)S(1)}, u32[]{:S(2)}, u32[]{:S(2)}) collective-permute-start(bf16[4,128,128]{2,1,0:T(8,128)(2,1)S(1)} %bitcast.280), channel_id=1, source_target_pairs={{0,16},{4,20},{8,24},{12,28},{16,0},{20,4},{24,8},{28,12},{1,17},{... | collective-permute-start | bytes 393224 | tf_op jit(solution)/shard_map/ppermute | solution.py:18
  26.3 9.6 %collective-permute-start.8 = (bf16[4,128,128]{2,1,0:T(8,128)(2,1)S(1)}, bf16[4,128,128]{2,1,0:T(8,128)(2,1)S(1)}, u32[]{:S(2)}, u32[]{:S(2)}) collective-permute-start(bf16[4,128,128]{2,1,0:T(8,128)(2,1)S(1)} %bitcast.278), channel_id=1, source_target_pairs={{0,16},{4,20},{8,24},{12,28},{16,0},{20,4},{24,8},{28,12},{1,17},{... | collective-permute-start | bytes 393224 | tf_op jit(solution)/shard_map/ppermute | solution.py:18
  27.9 9.4 %collective-permute-start.11 = (bf16[4,128,128]{2,1,0:T(8,128)(2,1)S(1)}, bf16[4,128,128]{2,1,0:T(8,128)(2,1)S(1)}, u32[]{:S(2)}, u32[]{:S(2)}) collective-permute-start(bf16[4,128,128]{2,1,0:T(8,128)(2,1)S(1)} %bitcast.282), channel_id=1, source_target_pairs={{0,16},{4,20},{8,24},{12,28},{16,0},{20,4},{24,8},{28,12},{1,17},{... | collective-permute-start | bytes 393224 | tf_op jit(solution)/shard_map/ppermute | solution.py:18
  38.3 39.6 %copy-start.2 = (bf16[6,128,128]{2,1,0:T(8,128)(2,1)S(1)}, bf16[6,128,128]{2,1,0:T(8,128)(2,1)}, u32[]{:S(2)}) copy-start(bf16[6,128,128]{2,1,0:T(8,128)(2,1)} %param.10) | copy-start | bytes 589828
  38.3 101.8 %all-reduce.5.cloned.1.call-start = ((), (), s32[]{:S(2)}) async-start(), calls=%async_computation | async-start | bytes 1310720 | tf_op jit(solution)/shard_map/psum | solution.py:119
  76.1 1.8 %copy-start.1 = (f32[128,128]{0,1:T(8,128)S(1)}, f32[128,128]{0,1:T(8,128)}, u32[]{:S(2)}) copy-start(f32[128,128]{0,1:T(8,128)} %get-tuple-element.10) | copy-start | bytes 196612
  76.1 1.8 %copy-start.9 = (f32[128,128]{0,1:T(8,128)S(1)}, f32[128,128]{0,1:T(8,128)}, u32[]{:S(2)}) copy-start(f32[128,128]{0,1:T(8,128)} %get-tuple-element.11) | copy-start | bytes 196612
  77.9 0.8 copy-start.8
  80.6 0.8 copy-start.7
  84.6 55.5 %copy-start.4 = (f32[4,128,128]{2,1,0:T(8,128)S(1)}, f32[4,128,128]{2,1,0:T(8,128)}, u32[]{:S(2)}) copy-start(f32[4,128,128]{2,1,0:T(8,128)} %param.11) | copy-start | bytes 786436
  140.1 1.0 copy-start.6
  141.1 0.9 copy-start.5
  142.6 1.0 copy-start.3
Sparse Core Ops, SparseCore 0:
  38.4 37.6 all-reduce.6
  84.7 55.3 all-reduce.4
